TPU v7x, 256 devices: a whole 4x4x8 slice. The times are simulated.
256 devices in a mesh: role: 2 (over x_hi), seq: 16 (over z, core), head: 8 (over x_lo, y).
Axes of the slice: x: 4 (x_hi: 2, x_lo: 2; x = x_hi * 2 + x_lo), y: 4, z: 8, core: 2. Of those that a mesh axis runs over, the one named last changes fastest.
Arguments:
- hidden_rows: bfloat16 [6144, 5120], P('seq'), may hold values from -6 to 6
- gen_weight: bfloat16 [5120, 5120], P(None, ('role', 'head')), may hold values from -0.078125 to 0.078125
- noise: bfloat16 [6144, 5120], P('seq'), may hold values from -6 to 6
- timesteps: int32 [96], P('seq'), may hold values from 20 to 979
- qkv_weight: bfloat16 [2, 5120, 9216], P('role', 'seq', 'head'), may hold values from -0.078125 to 0.078125
- out_weight: bfloat16 [2, 3072, 5120], P('role', 'head'), may hold values from -0.109375 to 0.109375
- qk_gain: float32 [2, 2, 24], P('role', None, 'head'), may hold values from 0.6 to 9
- block_keys: int32 [24, 96, 8], P('head', 'seq'), may hold values from 0 to 95, as said below
- block_count: int32 [24, 96], P('head', 'seq'), may hold values from 1 to 8, as said below
Outputs:
- score_grad: float32 [6144, 5120], P('seq', ('role', 'head'))
Inputs may be any that keep to these rules, and one draw needn't show every extreme that they name: `block_keys`: entry 0 of each list is the query block itself; the entries of one list are distinct. For each head, all entries of the lists of one index of seq name at most 2 distinct blocks of any other index of seq, and every index names exactly 2 blocks of the next index. `block_count`: in every draw the lists of some sequence shards are all full, those of others shorter.
All inputs are finite; a program needn't handle non-finite values.
Results may differ from a plain program's by a relative error of at most 0.018.
The roundings to bfloat16 on the way count: a program that leaves them out, or rounds other values in their place, can miss the bound.
Values may be sent and summed in bfloat16 or wider, within the bound.
A program may use at most 128 MiB of HBM per device.

v0:
```python
import math

import jax
import jax.numpy as jnp
from jax import lax
from jax.sharding import PartitionSpec as P

HEAD_DIM = 128
BLOCK = 64
KMAX = 8


def rms_rows(values):
    return values * lax.rsqrt(jnp.mean(values * values, axis=-1, keepdims=True) + 1e-06)


def block_attention(queries, key_table, value_table, key_list, key_count):
    picked_keys = key_table[key_list]
    picked_values = value_table[key_list]
    scale = 1.0 / math.sqrt(HEAD_DIM)
    scores = (
        jnp.einsum("nqe,nkbe->nqkb", queries, picked_keys, preferred_element_type=jnp.float32)
        * scale
    )
    live = lax.broadcasted_iota(jnp.int32, (key_list.shape[0], KMAX), 1) < key_count[:, None]
    scores = jnp.where(live[:, None, :, None], scores, -jnp.inf)
    highest = jnp.max(scores, axis=(2, 3), keepdims=True)
    raised = jnp.exp(scores - highest)
    summed = jnp.sum(raised, axis=(2, 3), keepdims=True)
    weights = (raised / summed).astype(jnp.bfloat16)
    mixed = jnp.einsum("nqkb,nkbe->nqe", weights, picked_values, preferred_element_type=jnp.float32)
    return mixed.astype(jnp.bfloat16)


def per_device(
    hidden_rows,
    gen_weight,
    noise,
    timesteps,
    qkv_weight,
    out_weight,
    qk_gain,
    block_keys,
    block_count,
):
    generated = jnp.dot(hidden_rows, gen_weight, preferred_element_type=jnp.float32).astype(
        jnp.bfloat16
    )
    forked = lax.all_gather(generated, ("role", "head"), axis=1, tiled=True)
    row_count = forked.shape[0]
    width = forked.shape[1]
    local_blocks = timesteps.shape[0]
    angle_blocks = (timesteps.astype(jnp.float32) * (math.pi / 2000.0))[:, None, None]
    noisy = jnp.cos(angle_blocks) * forked.astype(jnp.float32).reshape(local_blocks, BLOCK, width)
    noisy = noisy + jnp.sin(angle_blocks) * noise.astype(jnp.float32).reshape(
        local_blocks, BLOCK, width
    )
    normed = rms_rows(noisy).reshape(row_count, width).astype(jnp.bfloat16)
    weight_here = qkv_weight[0]
    projected = jnp.dot(
        normed,
        lax.all_gather(weight_here, "seq", axis=0, tiled=True),
        preferred_element_type=jnp.float32,
    )
    heads_here = projected.shape[1] // (3 * HEAD_DIM)
    head_parts = projected.reshape(row_count, heads_here, 3, HEAD_DIM)
    gain_here = qk_gain[0]
    queries = (rms_rows(head_parts[:, :, 0]) * gain_here[0][None, :, None]).astype(jnp.bfloat16)
    key_local = (rms_rows(head_parts[:, :, 1]) * gain_here[1][None, :, None]).astype(jnp.bfloat16)
    value_local = head_parts[:, :, 2].astype(jnp.bfloat16)
    query_table = queries.reshape(local_blocks, BLOCK, heads_here, HEAD_DIM).transpose(2, 0, 1, 3)
    key_rows, value_rows = (
        lax.all_gather(
            key_local.reshape(row_count, heads_here * HEAD_DIM), "seq", axis=0, tiled=True
        ),
        lax.all_gather(
            value_local.reshape(row_count, heads_here * HEAD_DIM), "seq", axis=0, tiled=True
        ),
    )
    all_blocks = key_rows.shape[0] // BLOCK
    key_table = key_rows.reshape(all_blocks, BLOCK, heads_here, HEAD_DIM).transpose(2, 0, 1, 3)
    value_table = value_rows.reshape(all_blocks, BLOCK, heads_here, HEAD_DIM).transpose(2, 0, 1, 3)
    attended = jax.vmap(block_attention)(
        query_table, key_table, value_table, block_keys, block_count
    )
    attended = attended.transpose(1, 2, 0, 3).reshape(row_count, heads_here * HEAD_DIM)
    contribution = jnp.dot(attended, out_weight[0], preferred_element_type=jnp.float32)
    signed = (2.0 * lax.axis_index("role").astype(jnp.float32) - 1.0) * contribution
    return lax.psum_scatter(
        signed.astype(jnp.bfloat16), ("role", "head"), scatter_dimension=1, tiled=True
    ).astype(jnp.float32)


def solution(mesh):
    placed = (
        P("seq", None),
        P(None, ("role", "head")),
        P("seq", None),
        P("seq"),
        P("role", "seq", "head"),
        P("role", "head", None),
        P("role", None, "head"),
        P("head", "seq", None),
        P("head", "seq"),
    )
    return jax.shard_map(
        per_device,
        mesh=mesh,
        in_specs=placed,
        out_specs=P("seq", ("role", "head")),
        check_vma=False,
    )
```

profile of v0, /device:TPU:2, one launch (start us, length us, event | category | flops | bytes accessed | tf_op | source)
XLA Modules:
  0.0 392.9 jit_solution(4628100102060441840)
XLA Ops:
  6.5 1.9 copy-done
  8.5 4.7 %convolution_convert_fusion = bf16[384,320]{0,1:T(8,128)(2,1)} fusion(bf16[384,5120]{1,0:T(8,128)(2,1)} %param.9, bf16[5120,320]{0,1:T(8,128)(2,1)S(1)} %copy-done), kind=kOutput, calls=%fused_computation.21 | convolution fusion | flops 1258414080 | bytes 7454720 | tf_op jit(solution)/shard_map/dot_general | solution.py:46
  14.3 6.3 %copy.26 = bf16[384,5120]{0,1:T(8,128)(2,1)} copy(bf16[384,5120]{1,0:T(8,128)(2,1)} %param.11) | data formatting | bytes 7864320 | tf_op args[2]
  20.6 50.8 %all-gather.6.cloned.1.call-done = bf16[384,5120]{0,1:T(8,128)(2,1)} async-done(((bf16[384,320]{0,1:T(8,128)(2,1)}), bf16[384,5120]{0,1:T(8,128)(2,1)}) %all-gather.6.cloned.1.call-update) | async-done | bytes 3932176 | tf_op jit(solution)/shard_map/all_gather | solution.py:49
  71.4 5.2 %multiply_reduce_fusion = f32[384]{0:T(512)S(1)} fusion(bf16[384,5120]{0,1:T(8,128)(2,1)} %copy.26, bf16[384,5120]{0,1:T(8,128)(2,1)} %all-gather.6.cloned.1.call-done, f32[384]{0:T(512)S(1)} %mul.117, f32[384]{0:T(512)S(1)} %mul.113), kind=kLoop, calls=%fused_computation.4 | loop fusion | flops 13762176 | bytes 7868928 | tf_op jit(solution)/shard_map/reduce_sum | solution.py:14
  76.6 68.3 %all-gather.12.cloned.1.call-done = bf16[1,5120,1152]{2,1,0:T(8,128)(2,1)} async-done(((bf16[1,320,1152]{2,1,0:T(8,128)(2,1)}), bf16[1,5120,1152]{2,1,0:T(8,128)(2,1)}) %all-gather.12.cloned.1.call-update) | async-done | bytes 11796496 | tf_op jit(solution)/shard_map/all_gather | solution.py:62
  144.9 15.6 %copy.27 = bf16[1152,5120]{1,0:T(8,128)(2,1)} copy(bf16[1152,5120]{0,1:T(8,128)(2,1)} %bitcast.71) | data formatting | bytes 23592960 | tf_op jit(solution)/shard_map/dot_general | solution.py:60
  160.5 11.7 %fusion.2 = f32[384,3,3,128]{0,3,2,1:T(8,128)S(1)} fusion(bf16[3,3,128,5120]{3,2,1,0:T(8,128)(2,1)} %bitcast.72, bf16[384,5120]{0,1:T(8,128)(2,1)} %copy.26, bf16[384,5120]{0,1:T(8,128)(2,1)} %all-gather.6.cloned.1.call-done, f32[384]{0:T(512)S(1)} %add_rsqrt_fusion.2, f32[384]{0:T(512)S(1)} %mul.117, f32[384]{0:T(512)S(1)} %mul.113), kind=kOutput, calls=%fused_computation.12 | convolution fusion | flops 4543610880 | bytes 21434880 | tf_op jit(solution)/shard_map/dot_general | solution.py:60
  172.2 0.9 copy.32
  173.5 0.8 fusion.14
  175.1 39.0 %all-gather.10.cloned.1.call-done = bf16[6144,384]{1,0:T(8,128)(2,1)} async-done(((bf16[384,384]{1,0:T(8,128)(2,1)}), bf16[6144,384]{1,0:T(8,128)(2,1)}) %all-gather.10.cloned.1.call-update) | async-done | bytes 4718608 | tf_op jit(solution)/shard_map/all_gather | solution.py:76
  214.1 12.9 %reshape.83 = bf16[96,64,3,128]{3,2,1,0:T(4,128)(2,1)} reshape(bf16[6144,384]{1,0:T(8,128)(2,1)} %all-gather.10.cloned.1.call-done) | data formatting | bytes 9437184 | tf_op jit(solution)/shard_map/reshape | solution.py:82
  227.0 6.4 %copy.49 = bf16[96,64,3,128]{3,1,0,2:T(8,128)(2,1)} copy(bf16[96,64,3,128]{3,2,1,0:T(4,128)(2,1)} %reshape.83) | data formatting | bytes 9437184 | tf_op jit(solution)/shard_map/reshape | solution.py:82
  233.4 24.2 %all-gather.8.cloned.1.call-done = bf16[6144,384]{0,1:T(8,128)(2,1)} async-done(((bf16[384,384]{0,1:T(8,128)(2,1)}), bf16[6144,384]{0,1:T(8,128)(2,1)}) %all-gather.8.cloned.1.call-update) | async-done | bytes 4718608 | tf_op jit(solution)/shard_map/all_gather | solution.py:73
  257.6 13.8 %reshape.106 = bf16[96,64,3,128]{1,0,3,2:T(8,128)(2,1)} reshape(bf16[6144,384]{0,1:T(8,128)(2,1)} %all-gather.8.cloned.1.call-done) | data formatting | bytes 9437184 | tf_op jit(solution)/shard_map/reshape | solution.py:81
  271.5 12.8 %copy.31 = bf16[96,64,3,128]{3,1,0,2:T(8,128)(2,1)} copy(bf16[96,64,3,128]{1,0,3,2:T(8,128)(2,1)} %reshape.106) | data formatting | bytes 9437184 | tf_op jit(solution)/shard_map/reshape | solution.py:81
  284.3 5.7 %gather_fusion.1 = bf16[144,64,128]{2,1,0:T(8,128)(2,1)} fusion(bf16[3,96,64,128]{3,2,1,0:T(8,128)(2,1)} %bitcast.74, s32[144]{0:T(256)S(1)} %reshape.85), kind=kCustom, calls=%fused_computation.1 | custom fusion | bytes 4719744 | tf_op jit(solution)/shard_map/vmap()/gather | solution.py:19
  290.0 4.4 %gather_fusion = bf16[144,64,128]{2,1,0:T(8,128)(2,1)S(1)} fusion(bf16[3,96,64,128]{3,2,1,0:T(8,128)(2,1)} %bitcast.73, s32[144]{0:T(256)S(1)} %reshape.85), kind=kCustom, calls=%fused_computation | custom fusion | bytes 4719744 | tf_op jit(solution)/shard_map/vmap()/gather | solution.py:18
  294.4 1.0 fusion
  295.4 1.3 fusion.8
  297.1 1.9 fusion.12
  299.3 4.2 %multiply_convert_fusion = bf16[384,5120]{0,1:T(8,128)(2,1)} fusion(bf16[1,384,5120]{2,1,0:T(8,128)(2,1)S(1)} %copy-done.6, f32[]{:T(128)S(6)} %sub.11, bf16[48,8,3,128]{3,2,1,0:T(4,128)(2,1)S(1)} %bitcast.78), kind=kOutput, calls=%fused_computation.2 | convolution fusion | flops 1513881600 | bytes 8159236 | tf_op jit(solution)/shard_map/dot_general | solution.py:87
  303.4 81.1 %reduce-scatter.2.cloned.1.call-done = bf16[384,320]{0,1:T(8,128)(2,1)} async-done(((bf16[384,5120]{0,1:T(8,128)(2,1)}), bf16[384,320]{0,1:T(8,128)(2,1)}) %reduce-scatter.2.cloned.1.call-update) | async-done | bytes 245776 | tf_op jit(solution)/shard_map/reduce_scatter | solution.py:89
  384.6 1.8 convert_element_type.60
  (43 shorter events, 2.8 us)
Async XLA Ops:
  6.5 1.9 copy-start
  6.5 7.4 %copy-start.7 = (s32[6]{0:T(128)S(1)}, s32[6]{0:T(128)}, u32[]{:S(2)}) copy-start(s32[6]{0:T(128)} %param.12) | copy-start | bytes 76
  6.5 64.9 %all-gather.6.cloned.1.call-start = ((), (), s32[]{:S(2)}) async-start(), calls=%async_computation.1 | async-start | bytes 4177920 | tf_op jit(solution)/shard_map/all_gather | solution.py:49
  13.2 131.7 %all-gather.12.cloned.1.call-start = ((), (), s32[]{:S(2)}) async-start(), calls=%async_computation.5 | async-start | bytes 12533760 | tf_op jit(solution)/shard_map/all_gather | solution.py:62
  13.9 200.2 %all-gather.10.cloned.1.call-start = ((), (), s32[]{:S(2)}) async-start(), calls=%async_computation.3 | async-start | bytes 5013504 | tf_op jit(solution)/shard_map/all_gather | solution.py:76
  160.5 12.7 %copy-start.5 = (f32[1,2,3]{2,1,0:T(2,128)S(1)}, f32[1,2,3]{2,1,0:T(2,128)}, u32[]{:S(2)}) copy-start(f32[1,2,3]{2,1,0:T(2,128)} %param.15) | copy-start | bytes 76
  172.2 2.4 copy-start.3
  172.2 2.5 copy-start.4
  173.2 84.5 %all-gather.8.cloned.1.call-start = ((), (), s32[]{:S(2)}) async-start(), calls=%async_computation.2 | async-start | bytes 5013504 | tf_op jit(solution)/shard_map/all_gather | solution.py:73
  174.3 210.2 %reduce-scatter.2.cloned.1.call-start = ((), (), s32[]{:S(2)}) async-start(), calls=%async_computation.4 | async-start | bytes 4177920 | tf_op jit(solution)/shard_map/reduce_scatter | solution.py:89
  295.4 1.7 copy-start.2
  297.1 2.2 copy-start.6
  299.2 87.1 %copy-start.1 = (bf16[5120,320]{0,1:T(8,128)(2,1)S(1)}, bf16[5120,320]{0,1:T(8,128)(2,1)}, u32[]{:S(2)}) copy-start(bf16[5120,320]{0,1:T(8,128)(2,1)} %param.10) | copy-start | bytes 9830404
Sparse Core Ops, SparseCore 0:
  13.3 58.0 all-gather.5
  73.3 71.6 all-gather.11
  173.3 40.7 all-gather.9
  215.7 41.8 all-gather.7
  303.6 80.9 reduce-scatter.1
where the time goes:
time: 395 us; the launch traced here: 393 us
  waiting for transfers between devices  264 us (67%)
  local copies, waits for them, and re-layouts  82.2 us (21%)
  matrix products  23.4 us (6%)
  between operations  13.3 us (3%)
  other arithmetic  9.34 us (2%)
    reduce_scatter x1, waiting for transfers between devices, per_device(): lax.psum_scatter(signed.astype(jnp.bfloat16), ('role', 'head'), scatter_d...  81.1 us
    all_gather x1, waiting for transfers between devices, per_device(): lax.all_gather(weight_here, 'seq', axis=0, tiled=True)  68.3 us
    all_gather x1, waiting for transfers between devices, per_device(): forked = lax.all_gather(generated, ('role', 'head'), axis=1, tiled=True)  50.8 us
    all_gather x1, waiting for transfers between devices, per_device(): lax.all_gather(value_local.reshape(row_count, heads_here * HEAD_DIM), 'se...  39 us
    reshape x2, local copies, waits for them, and re-layouts, per_device(): key_rows.reshape(all_blocks, BLOCK, heads_here, HEAD_DIM)  26.6 us
    all_gather x1, waiting for transfers between devices, per_device(): lax.all_gather(key_local.reshape(row_count, heads_here * HEAD_DIM), 'seq'...  24.2 us
    reshape x2, local copies, waits for them, and re-layouts, per_device(): value_rows.reshape(all_blocks, BLOCK, heads_here, HEAD_DIM)  19.3 us
    dot_general x1, local copies, waits for them, and re-layouts, per_device(): jnp.dot(normed, lax.all_gather(weight_here, 'seq', axis=0, tiled=True), p...  15.6 us
  transfers between devices with their start and end apart: 5, of which 5 were waited for; matrix products, arithmetic and copies ran while one was open for 8% of the time, Pallas kernels for 0%

commit v1 on v0

v1 whole, which is shorter than its diff:
```python
import math

import jax
import jax.numpy as jnp
from jax import lax
from jax.experimental import pallas as pl
from jax.experimental.pallas import tpu as pltpu
from jax.sharding import PartitionSpec as P

HEAD_DIM = 128
BLOCK = 64
KMAX = 8
ROWS = 384
D = 5120
SLICE = 320
NX, NY, NZ = 4, 4, 8
HEADS_HERE = 3
MESH = pl.DeviceIdType.MESH
F32 = jnp.float32
BF16 = jnp.bfloat16


def rms(values):
    return values * lax.rsqrt(jnp.mean(values * values, axis=-1, keepdims=True) + 1e-06)


def kernel(
    angles, gain, keys, count,
    hidden, gen_w, noise, qkv_w, out_w,
    out,
    hid, gw, nz, xg, wb, qt, kv0, kv1, kv2, sl, wo, at, acc, oacc,
    loc_sem, zs, zr, ps, pr, xs, xr, ws, wr,
):
    kv = (kv0, kv1, kv2)
    role = lax.axis_index("role")
    seq = lax.axis_index("seq")
    head = lax.axis_index("head")
    z, c = seq // 2, seq % 2
    x = role * 2 + head // 4
    y = head % 4
    me = x * NY + y

    def at_x(d):
        xx = (x + d + NX) % NX
        return {"role": xx // 2, "head": (xx % 2) * 4 + y}

    def at_y(d):
        return {"head": (head // 4) * 4 + (y + d + NY) % NY}

    def at_z(d):
        return {"seq": ((z + d + NZ) % NZ) * 2 + c}

    def plane(i):
        j = (me + i) % 16
        return {"role": j // 8, "head": j % 8}

    partner = {"seq": z * 2 + 1 - c}

    def local(src, dst, i):
        cp = pltpu.make_async_copy(src, dst, loc_sem.at[i])
        cp.start()
        return cp

    w_own = [
        local(qkv_w.at[0, :, pl.ds(h * ROWS, ROWS)], wb.at[h, z, c], h)
        for h in range(HEADS_HERE)
    ]
    hid_cp = local(hidden, hid, 3)
    gw_cp = local(gen_w, gw, 4)
    nz_cp = local(noise, nz, 5)

    barrier = pltpu.get_barrier_semaphore()
    for d in (1, -1):
        pl.semaphore_signal(barrier, inc=1, device_id=at_z(d), device_id_type=MESH)
    pl.semaphore_signal(barrier, inc=1, device_id=partner, device_id_type=MESH)

    def greet(i, carry):
        pl.semaphore_signal(barrier, inc=1, device_id=plane(i), device_id_type=MESH)
        return carry

    lax.fori_loop(1, 16, greet, 0)
    pl.semaphore_wait(barrier, 18)

    started = []

    def send(src, dst, ssem, rsem, device):
        cp = pltpu.make_async_remote_copy(
            src_ref=src, dst_ref=dst, send_sem=ssem, recv_sem=rsem,
            device_id=device, device_id_type=MESH,
        )
        cp.start()
        started.append(cp)
        return cp

    class Ring:
        def __init__(self, g, part, whole):
            self.g, self.part, self.whole = g, part, whole
            self.cp = {}

        def push(self, way, half, k):
            shard = (z + NZ - way * (k - 1)) % NZ
            i = (0 if way > 0 else 7) + (k - 1 if half == 0 else (4 if way > 0 else 3) + k - 1)
            ref = self.part(shard, half)
            self.cp[way, half, k] = send(
                ref, ref, zs.at[self.g, i], zr.at[self.g, i], at_z(way)
            )

        def give(self, d):
            ref = self.whole((z + d + NZ) % NZ)
            n = d + 3
            self.cp["p", d] = send(ref, ref, ps.at[self.g, n], pr.at[self.g, n], partner)

        def own(self):
            self.push(1, 0, 1)
            self.push(-1, 1, 1)
            self.push(1, 1, 1)
            self.push(-1, 0, 1)
            self.give(0)

        def step(self, k):
            if k < 4:
                for way, half in ((1, 0), (-1, 1)):
                    self.cp[way, half, k].wait_recv()
                    self.push(way, half, k + 1)
                for way, half in ((1, 1), (-1, 0)):
                    self.cp[way, half, k].wait_recv()
                    if k < 3:
                        self.push(way, half, k + 1)
                self.give(-k)
                self.give(k)
            else:
                self.cp[1, 0, 4].wait_recv()
                self.cp[-1, 1, 4].wait_recv()
                self.give(4)

        def finish(self):
            for d in range(-3, 5):
                self.cp["p", d].wait_recv()

    def w_ring(h):
        return Ring(
            h,
            lambda zz, half: wb.at[h, zz, c, pl.ds(half * 160, 160)],
            lambda zz: wb.at[h, zz, c],
        )

    def kv_ring(h):
        return Ring(
            3 + h,
            lambda zz, half: kv[h].at[zz, c, pl.ds(half * 3, 3)],
            lambda zz: kv[h].at[zz, c],
        )

    class Plane:
        def __init__(self, g, buf):
            self.g, self.buf = g, buf
            self.n = 0
            self.cp = {}

        def push(self, name, ref, device):
            self.cp[name] = send(
                ref, ref, xs.at[self.g, self.n], xr.at[self.g, self.n], device
            )
            self.n += 1

        def start(self):
            b = self.buf
            for d in (1, -1):
                self.push(("a1", d), b.at[x, y, pl.ds(0, 192)], at_x(d))
                self.push(("b1", d), b.at[x, y, pl.ds(192, 192)], at_y(d))

        def one(self):
            b = self.buf
            for n, d in enumerate((1, -1)):
                self.cp["a1", d].wait_recv()
                self.push(("a2", d), b.at[(x - d + NX) % NX, y, pl.ds(n * 96, 96)], at_x(d))
                self.cp["b1", d].wait_recv()
                self.push(("b2", d), b.at[x, (y - d + NY) % NY, pl.ds(192 + n * 96, 96)], at_y(d))

        def two(self):
            b = self.buf
            for d in (1, -1):
                self.cp["a2", d].wait_recv()
            for d in (1, -1):
                self.push(("a3", d), b.at[:, y, pl.ds(0, 192)], at_y(d))
            for d in (1, -1):
                self.cp["b2", d].wait_recv()
            for d in (1, -1):
                self.push(("b3", d), b.at[x, :, pl.ds(192, 192)], at_x(d))

        def three(self):
            b = self.buf
            for n, d in enumerate((1, -1)):
                self.cp["a3", d].wait_recv()
                self.push(
                    ("a4", d), b.at[pl.ds(2 * n, 2), (y - d + NY) % NY, pl.ds(0, 192)], at_y(d)
                )
                self.cp["b3", d].wait_recv()
                self.push(
                    ("b4", d), b.at[(x - d + NX) % NX, pl.ds(2 * n, 2), pl.ds(192, 192)], at_x(d)
                )

        def four(self):
            for d in (1, -1):
                self.cp["a4", d].wait_recv()
                self.cp["b4", d].wait_recv()

    wr_ = [w_ring(h) for h in range(HEADS_HERE)]
    kr_ = [kv_ring(h) for h in range(HEADS_HERE)]
    gx = Plane(0, xg)
    ax = [Plane(1 + h, at.at[h]) for h in range(HEADS_HERE)]

    for h in range(HEADS_HERE):
        w_own[h].wait()
        if h < 2:
            wr_[h].own()

    hid_cp.wait()
    gw_cp.wait()
    acc[:, :SLICE] = jnp.zeros((ROWS, SLICE), F32)

    def gen_step(i, carry):
        k0 = pl.multiple_of(i * 1024, 1024)
        acc[:, :SLICE] += jnp.dot(
            hid[:, pl.ds(k0, 1024)], gw[pl.ds(k0, 1024), :], preferred_element_type=F32
        )
        return carry

    lax.fori_loop(0, D // 1024, gen_step, 0)
    xg[x, y] = acc[:, :SLICE].astype(BF16)
    gx.start()
    wr_[0].step(1)
    ow_cp = local(out_w.at[0], hid, 6)
    gx.one()
    wr_[1].step(1)
    gx.two()

    ow_cp.wait()
    for j in range(16):
        sl[j] = hid[:, j * SLICE:(j + 1) * SLICE].reshape(HEADS_HERE, 128, SLICE)

    wr_[0].step(2)
    wr_[2].own()
    wr_[1].step(2)
    gx.three()
    gx.four()

    half = pl.ds(c * 64, 64)
    wo_own = pltpu.make_async_copy(sl.at[me, :, half], wo.at[:, me, half], loc_sem.at[7])
    wo_own.start()

    def wo_copy(i):
        j = (me + i) % 16
        return pltpu.make_async_remote_copy(
            src_ref=sl.at[j, :, half], dst_ref=wo.at[:, me, half],
            send_sem=ws.at[i], recv_sem=wr.at[i],
            device_id=plane(i), device_id_type=MESH,
        )

    def wo_start(i, carry):
        wo_copy(i).start()
        return carry

    lax.fori_loop(1, 16, wo_start, 0)

    nz_cp.wait()
    for cp in gx.cp.values():
        cp.wait_send()
    drained = {id(cp) for cp in gx.cp.values()}

    def norm_step(b, carry):
        rows = pl.ds(pl.multiple_of(b * BLOCK, BLOCK), BLOCK)
        ca, sa = angles[0, b], angles[1, b]

        def noisy(j):
            g = xg[j // NY, j % NY, rows, :].astype(F32)
            n = nz[rows, j * SLICE:(j + 1) * SLICE].astype(F32)
            return ca * g + sa * n

        total = jnp.zeros((BLOCK, 1), F32)
        for j in range(16):
            v = noisy(j)
            total = total + jnp.sum(v * v, axis=-1, keepdims=True)
        inv = lax.rsqrt(total * (1.0 / D) + 1e-06)
        for j in range(16):
            xg[j // NY, j % NY, rows, :] = (noisy(j) * inv).astype(BF16)
        return carry

    lax.fori_loop(0, ROWS // BLOCK, norm_step, 0)

    def project(h):
        acc[...] = jnp.zeros((ROWS, ROWS), F32)

        def proj_step(zz, carry):
            part = jnp.zeros((ROWS, ROWS), F32)
            for cc in range(2):
                s = zz * 2 + cc
                part = part + jnp.dot(
                    xg[s // NY, s % NY], wb[h, zz, cc], preferred_element_type=F32
                )
            acc[...] += part
            return carry

        lax.fori_loop(0, NZ, proj_step, 0)
        q = (rms(acc[:, 0:128]) * gain[0, 0, h]).astype(BF16)
        k = (rms(acc[:, 128:256]) * gain[0, 1, h]).astype(BF16)
        v = acc[:, 256:384].astype(BF16)
        qt[h] = q.reshape(6, BLOCK, HEAD_DIM)
        kv[h][z, c, :, :, 0:128] = k.reshape(6, BLOCK, HEAD_DIM)
        kv[h][z, c, :, :, 128:256] = v.reshape(6, BLOCK, HEAD_DIM)

    sign = (2 * role - 1).astype(F32)
    scale = 1.0 / math.sqrt(HEAD_DIM)

    def attend(h):
        def two_blocks(b2, carry):
            for u in range(2):
                b = b2 * 2 + u
                q = qt[h, b]
                got = []
                for j in range(KMAX):
                    kb = keys[h, b, j]
                    s = kb // 6
                    got.append(kv[h][s // 2, s % 2, kb - s * 6])
                both = jnp.concatenate(got, axis=0)
                s = lax.dot_general(
                    q, both[:, 0:128], (((1,), (1,)), ((), ())), preferred_element_type=F32
                ) * scale
                limit = count[h, b] * BLOCK
                live = lax.broadcasted_iota(jnp.int32, (BLOCK, KMAX * BLOCK), 1) < limit
                s = jnp.where(live, s, -jnp.inf)
                raised = jnp.exp(s - jnp.max(s, axis=-1, keepdims=True))
                w = (raised / jnp.sum(raised, axis=-1, keepdims=True)).astype(BF16)
                mixed = jnp.dot(w, both[:, 128:256], preferred_element_type=F32)
                rows = pl.ds(pl.multiple_of(b * BLOCK, BLOCK), BLOCK)
                at[h, x, y, rows, :] = (mixed * sign).astype(BF16)
            return carry

        lax.fori_loop(0, 3, two_blocks, 0)

    def final(h):
        def final_step(i, carry):
            part = jnp.zeros((ROWS, SLICE), F32)
            for u in range(2):
                j = i * 4 + u * 2
                a = jnp.concatenate([at[h, i, u * 2], at[h, i, u * 2 + 1]], axis=-1)
                part = part + jnp.dot(
                    a, wo[h, pl.ds(j, 2)].reshape(256, SLICE), preferred_element_type=F32
                )
            oacc[...] += part
            return carry

        lax.fori_loop(0, 4, final_step, 0)

    oacc[...] = jnp.zeros((ROWS, SLICE), F32)
    wr_[0].step(3)
    wr_[1].step(3)
    wr_[0].step(4)
    wr_[1].step(4)
    wr_[2].step(1)
    wr_[0].finish()
    project(0)
    kr_[0].own()
    wr_[2].step(2)
    wr_[1].finish()
    project(1)
    kr_[1].own()
    wr_[2].step(3)
    kr_[0].step(1)
    wr_[2].step(4)
    kr_[0].step(2)
    wr_[2].finish()
    project(2)
    kr_[0].step(3)
    kr_[1].step(1)
    kr_[2].own()
    kr_[0].step(4)
    kr_[1].step(2)

    wo_own.wait()

    def wo_wait(i, carry):
        wo_copy(i).wait()
        return carry

    lax.fori_loop(1, 16, wo_wait, 0)
    wo_swap = send(wo.at[:, :, half], wo.at[:, :, half], ws.at[0], wr.at[0], partner)

    kr_[0].finish()
    attend(0)
    ax[0].start()
    kr_[1].step(3)
    kr_[2].step(1)
    ax[0].one()
    kr_[1].step(4)
    ax[0].two()
    kr_[2].step(2)
    kr_[1].finish()
    attend(1)
    ax[0].three()
    ax[1].start()
    kr_[2].step(3)
    ax[0].four()
    ax[1].one()
    ax[1].two()
    kr_[2].step(4)
    ax[1].three()
    wo_swap.wait_recv()
    kr_[2].finish()
    attend(2)
    ax[2].start()
    final(0)
    ax[2].one()
    ax[1].four()
    ax[2].two()
    final(1)
    ax[2].three()
    ax[2].four()
    final(2)
    out[...] = oacc[...]
    for cp in started:
        if id(cp) not in drained:
            cp.wait_send()


def per_device(
    hidden_rows,
    gen_weight,
    noise,
    timesteps,
    qkv_weight,
    out_weight,
    qk_gain,
    block_keys,
    block_count,
):
    turn = timesteps.astype(F32) * (math.pi / 2000.0)
    angles = jnp.stack([jnp.cos(turn), jnp.sin(turn)])
    smem = pl.BlockSpec(memory_space=pltpu.SMEM)
    hbm = pl.BlockSpec(memory_space=pl.ANY)
    dma = pltpu.SemaphoreType.DMA
    return pl.pallas_call(
        kernel,
        out_shape=jax.ShapeDtypeStruct((ROWS, SLICE), F32),
        in_specs=[smem] * 4 + [hbm] * 5,
        out_specs=pl.BlockSpec(memory_space=pltpu.VMEM),
        scratch_shapes=[
            pltpu.VMEM((ROWS, D), BF16),
            pltpu.VMEM((D, SLICE), BF16),
            pltpu.VMEM((ROWS, D), BF16),
            pltpu.VMEM((NX, NY, ROWS, SLICE), BF16),
            pltpu.VMEM((HEADS_HERE, NZ, 2, SLICE, ROWS), BF16),
            pltpu.VMEM((HEADS_HERE, 6, BLOCK, HEAD_DIM), BF16),
            *[pltpu.VMEM((NZ, 2, 6, BLOCK, 2 * HEAD_DIM), BF16)] * HEADS_HERE,
            pltpu.VMEM((16, HEADS_HERE, 128, SLICE), BF16),
            pltpu.VMEM((HEADS_HERE, 16, 128, SLICE), BF16),
            pltpu.VMEM((HEADS_HERE, NX, NY, ROWS, HEAD_DIM), BF16),
            pltpu.VMEM((ROWS, ROWS), F32),
            pltpu.VMEM((ROWS, SLICE), F32),
            dma((8,)),
            dma((6, 14)),
            dma((6, 14)),
            dma((6, 8)),
            dma((6, 8)),
            dma((4, 16)),
            dma((4, 16)),
            dma((16,)),
            dma((16,)),
        ],
        compiler_params=pltpu.CompilerParams(
            collective_id=0, has_side_effects=True, vmem_limit_bytes=67043328
        ),
    )(
        angles, qk_gain, block_keys, block_count,
        hidden_rows, gen_weight, noise, qkv_weight, out_weight,
    )


def solution(mesh):
    placed = (
        P("seq", None),
        P(None, ("role", "head")),
        P("seq", None),
        P("seq"),
        P("role", "seq", "head"),
        P("role", "head", None),
        P("role", None, "head"),
        P("head", "seq", None),
        P("head", "seq"),
    )
    return jax.shard_map(
        per_device,
        mesh=mesh,
        in_specs=placed,
        out_specs=P("seq", ("role", "head")),
        check_vma=False,
    )
```

time: 395 us -> 184 us (0.47)
  waiting for transfers between devices: 264 us -> 0 us
  Pallas kernels: 0 us -> 173 us
  local copies, waits for them, and re-layouts: 82.2 us -> 7.88 us
  matrix products: 23.4 us -> 0 us
  between operations: 13.3 us -> 0.01 us
  other arithmetic: 9.34 us -> 1.27 us
    all_gather x4 -> x0, waiting for transfers between devices: 182 us -> none  [the longest x1 68.3 us: per_device(): lax.all_gather(weight_here, 'seq', axis=0, tiled=True)]
    pallas_call x0 -> x1, Pallas kernels: none -> 173 us  [per_device(): pl.pallas_call(kernel, out_shape=jax.ShapeDtypeStruct((ROWS, SLICE), F32)...]
    reduce_scatter x1 -> x0, waiting for transfers between devices: 81.1 us -> none  [per_device(): lax.psum_scatter(signed.astype(jnp.bfloat16), ('role', 'head'), scatter_d...]
    reshape x4 -> x0, local copies, waits for them, and re-layouts: 46 us -> none  [the longest x2 26.6 us: per_device(): key_rows.reshape(all_blocks, BLOCK, heads_here, HEAD_DIM)]
    dot_general x5 -> x0, matrix products: 23.4 us -> none  [the longest x1 11.7 us: per_device(): jnp.dot(normed, lax.all_gather(weight_here, 'seq', axis=0, tiled=True), p...]
    dot_general x1 -> x0, local copies, waits for them, and re-layouts: 15.6 us -> none  [per_device(): jnp.dot(normed, lax.all_gather(weight_here, 'seq', axis=0, tiled=True), p...]
    gather x3 -> x0, local copies, waits for them, and re-layouts: 10.2 us -> none  [the longest x1 5.73 us: block_attention(): picked_values = value_table[key_list]]
    reduce_sum x3 -> x0, other arithmetic: 6.61 us -> none  [the longest x2 5.31 us: rms_rows(): jnp.mean(values * values, axis=-1, keepdims=True) + 1e-06]
  transfers between devices with their start and end apart: 5 -> 0, of which waited for: 5 -> 0; matrix products, arithmetic and copies ran while one was open for 8% -> 0% of each run, Pallas kernels for 0% -> 0%
where the time goes in v1:
time: 184 us; the launch traced here: 183 us
  Pallas kernels  173 us (94%)
  local copies, waits for them, and re-layouts  7.88 us (4%)
    pallas_call x1, Pallas kernels, per_device(): pl.pallas_call(kernel, out_shape=jax.ShapeDtypeStruct((ROWS, SLICE), F32)...  173 us
    unnamed x1, local copies, waits for them, and re-layouts  5.82 us

profile of v1, /device:TPU:2, one launch (start us, length us, event | category | flops | bytes accessed | tf_op | source)
XLA Modules:
  0.0 182.6 jit_solution(16579254545296054267)
XLA Ops:
  0.0 0.7 cosine_bitcast_fusion
  0.7 0.6 pad_maximum_fusion.angles
  1.3 5.8 %copy.10.gen_w = bf16[5120,320]{1,0:T(8,128)(2,1)} copy(bf16[5120,320]{0,1:T(8,128)(2,1)} %param.10) | data formatting | bytes 6553600 | tf_op args[1]
  7.1 173.5 %shard_map.91 = f32[384,320]{1,0:T(8,128)} custom-call(f32[2,6]{1,0:T(2,128)} %pad_maximum_fusion.angles, f32[1,2,3]{2,1,0:T(2,128)} %gain.1, s32[3,6,8]{2,1,0:T(8,128)} %keys.1, s32[3,6]{1,0:T(4,128)} %count.1, bf16[384,5120]{1,0:T(8,128)(2,1)} %hidden.1, bf16[5120,320]{1,0:T(8,128)(2,1)} %copy.10.gen_w, bf16[384,5120]{1,0:T(8,128)(2,1)} %noise.1, ...), custom_call_target="tpu_custom_call" | custom-call | tf_op jit(solution)/shard_map/pallas_call | solution.py:442
  180.6 2.1 %copy.11 = f32[384,320]{0,1:T(8,128)} copy(f32[384,320]{1,0:T(8,128)} %shard_map.91) | data formatting | bytes 983040 | tf_op jit(solution)/shard_map/pallas_call | solution.py:442

commit v2 on v1

--- a/solution.py
+++ b/solution.py
@@ -25,7 +25,7 @@
 
 
 def kernel(
-    angles, gain, keys, count,
+    steps, gain, keys, count,
     hidden, gen_w, noise, qkv_w, out_w,
     out,
     hid, gw, nz, xg, wb, qt, kv0, kv1, kv2, sl, wo, at, acc, oacc,
@@ -117,21 +117,21 @@
             self.push(-1, 0, 1)
             self.give(0)
 
-        def step(self, k):
-            if k < 4:
-                for way, half in ((1, 0), (-1, 1)):
-                    self.cp[way, half, k].wait_recv()
+        def step_a(self, k):
+            for way, half in ((1, 0), (-1, 1)):
+                self.cp[way, half, k].wait_recv()
+                if k < 4:
                     self.push(way, half, k + 1)
-                for way, half in ((1, 1), (-1, 0)):
-                    self.cp[way, half, k].wait_recv()
-                    if k < 3:
-                        self.push(way, half, k + 1)
-                self.give(-k)
-                self.give(k)
-            else:
-                self.cp[1, 0, 4].wait_recv()
-                self.cp[-1, 1, 4].wait_recv()
+            if k == 4:
                 self.give(4)
+
+        def step_b(self, k):
+            for way, half in ((1, 1), (-1, 0)):
+                self.cp[way, half, k].wait_recv()
+                if k < 3:
+                    self.push(way, half, k + 1)
+            self.give(-k)
+            self.give(k)
 
         def finish(self):
             for d in range(-3, 5):
@@ -210,44 +210,29 @@
     gx = Plane(0, xg)
     ax = [Plane(1 + h, at.at[h]) for h in range(HEADS_HERE)]
 
-    for h in range(HEADS_HERE):
-        w_own[h].wait()
-        if h < 2:
-            wr_[h].own()
-
-    hid_cp.wait()
-    gw_cp.wait()
-    acc[:, :SLICE] = jnp.zeros((ROWS, SLICE), F32)
-
     def gen_step(i, carry):
         k0 = pl.multiple_of(i * 1024, 1024)
-        acc[:, :SLICE] += jnp.dot(
-            hid[:, pl.ds(k0, 1024)], gw[pl.ds(k0, 1024), :], preferred_element_type=F32
+        acc[:, :SLICE] += lax.dot_general(
+            hid[:, pl.ds(k0, 1024)], gw[:, pl.ds(k0, 1024)],
+            (((1,), (1,)), ((), ())), preferred_element_type=F32,
         )
         return carry
 
-    lax.fori_loop(0, D // 1024, gen_step, 0)
-    xg[x, y] = acc[:, :SLICE].astype(BF16)
-    gx.start()
-    wr_[0].step(1)
-    ow_cp = local(out_w.at[0], hid, 6)
-    gx.one()
-    wr_[1].step(1)
-    gx.two()
-
-    ow_cp.wait()
-    for j in range(16):
-        sl[j] = hid[:, j * SLICE:(j + 1) * SLICE].reshape(HEADS_HERE, 128, SLICE)
-
-    wr_[0].step(2)
-    wr_[2].own()
-    wr_[1].step(2)
-    gx.three()
-    gx.four()
+    def generate():
+        hid_cp.wait()
+        gw_cp.wait()
+        acc[:, :SLICE] = jnp.zeros((ROWS, SLICE), F32)
+        lax.fori_loop(0, D // 1024, gen_step, 0)
+        xg[x, y] = acc[:, :SLICE].astype(BF16)
+        held.append(local(out_w.at[0], hid, 6))
+
+    def cut():
+        held.pop().wait()
+        for j in range(16):
+            sl[j] = hid[:, j * SLICE:(j + 1) * SLICE].reshape(HEADS_HERE, 128, SLICE)
 
     half = pl.ds(c * 64, 64)
     wo_own = pltpu.make_async_copy(sl.at[me, :, half], wo.at[:, me, half], loc_sem.at[7])
-    wo_own.start()
 
     def wo_copy(i):
         j = (me + i) % 16
@@ -261,16 +246,23 @@
         wo_copy(i).start()
         return carry
 
-    lax.fori_loop(1, 16, wo_start, 0)
-
-    nz_cp.wait()
-    for cp in gx.cp.values():
-        cp.wait_send()
-    drained = {id(cp) for cp in gx.cp.values()}
+    def wo_wait(i, carry):
+        wo_copy(i).wait()
+        return carry
+
+    def swap_start():
+        wo_own.start()
+        lax.fori_loop(1, 16, wo_start, 0)
+
+    def swap_end():
+        wo_own.wait()
+        lax.fori_loop(1, 16, wo_wait, 0)
+        held.append(send(wo.at[:, :, half], wo.at[:, :, half], ws.at[0], wr.at[0], partner))
 
     def norm_step(b, carry):
         rows = pl.ds(pl.multiple_of(b * BLOCK, BLOCK), BLOCK)
-        ca, sa = angles[0, b], angles[1, b]
+        turn = jnp.full((8, SLICE), steps[b], jnp.int32).astype(F32) * (math.pi / 2000.0)
+        ca, sa = jnp.cos(turn)[0:1], jnp.sin(turn)[0:1]
 
         def noisy(j):
             g = xg[j // NY, j % NY, rows, :].astype(F32)
@@ -286,7 +278,11 @@
             xg[j // NY, j % NY, rows, :] = (noisy(j) * inv).astype(BF16)
         return carry
 
-    lax.fori_loop(0, ROWS // BLOCK, norm_step, 0)
+    def norm():
+        nz_cp.wait()
+        for cp in gx.cp.values():
+            cp.wait_send()
+        lax.fori_loop(0, ROWS // BLOCK, norm_step, 0)
 
     def project(h):
         acc[...] = jnp.zeros((ROWS, ROWS), F32)
@@ -352,72 +348,101 @@
 
         lax.fori_loop(0, 4, final_step, 0)
 
+    held = []
+    for h in range(HEADS_HERE):
+        w_own[h].wait()
     oacc[...] = jnp.zeros((ROWS, SLICE), F32)
-    wr_[0].step(3)
-    wr_[1].step(3)
-    wr_[0].step(4)
-    wr_[1].step(4)
-    wr_[2].step(1)
+    wr_[0].own()
+    generate()
+    gx.start()
+    cut()
+    wr_[0].step_a(1)
+    wr_[0].step_b(1)
+    wr_[1].own()
+    gx.one()
+    wr_[0].step_a(2)
+    gx.two()
+    wr_[0].step_b(2)
+    wr_[1].step_a(1)
+    wr_[1].step_b(1)
+    wr_[0].step_a(3)
+    wr_[0].step_b(3)
+    wr_[2].own()
+    wr_[1].step_a(2)
+    gx.three()
+    wr_[1].step_b(2)
+    wr_[0].step_a(4)
+    wr_[2].step_a(1)
     wr_[0].finish()
+    gx.four()
+    norm()
+    wr_[1].step_a(3)
+    wr_[1].step_b(3)
+    wr_[2].step_b(1)
     project(0)
+    wr_[2].step_a(2)
     kr_[0].own()
-    wr_[2].step(2)
+    swap_start()
+    wr_[1].step_a(4)
+    wr_[2].step_b(2)
+    wr_[2].step_a(3)
     wr_[1].finish()
     project(1)
+    kr_[0].step_a(1)
+    kr_[0].step_b(1)
     kr_[1].own()
-    wr_[2].step(3)
-    kr_[0].step(1)
-    wr_[2].step(4)
-    kr_[0].step(2)
+    wr_[2].step_b(3)
+    wr_[2].step_a(4)
+    kr_[0].step_a(2)
+    kr_[0].step_b(2)
+    kr_[1].step_a(1)
     wr_[2].finish()
     project(2)
-    kr_[0].step(3)
-    kr_[1].step(1)
+    kr_[0].step_a(3)
+    kr_[1].step_b(1)
     kr_[2].own()
-    kr_[0].step(4)
-    kr_[1].step(2)
-
-    wo_own.wait()
-
-    def wo_wait(i, carry):
-        wo_copy(i).wait()
-        return carry
-
-    lax.fori_loop(1, 16, wo_wait, 0)
-    wo_swap = send(wo.at[:, :, half], wo.at[:, :, half], ws.at[0], wr.at[0], partner)
-
+    kr_[0].step_b(3)
+    kr_[1].step_a(2)
+    kr_[0].step_a(4)
+    kr_[1].step_b(2)
     kr_[0].finish()
     attend(0)
+    kr_[2].step_a(1)
+    kr_[2].step_b(1)
     ax[0].start()
-    kr_[1].step(3)
-    kr_[2].step(1)
+    kr_[1].step_a(3)
+    swap_end()
     ax[0].one()
-    kr_[1].step(4)
+    kr_[1].step_b(3)
     ax[0].two()
-    kr_[2].step(2)
+    kr_[2].step_a(2)
+    kr_[2].step_b(2)
+    kr_[1].step_a(4)
+    kr_[2].step_a(3)
+    ax[0].three()
+    kr_[2].step_b(3)
+    kr_[2].step_a(4)
+    ax[0].four()
+    held.pop().wait_recv()
+    final(0)
     kr_[1].finish()
     attend(1)
-    ax[0].three()
     ax[1].start()
-    kr_[2].step(3)
-    ax[0].four()
-    ax[1].one()
-    ax[1].two()
-    kr_[2].step(4)
-    ax[1].three()
-    wo_swap.wait_recv()
     kr_[2].finish()
     attend(2)
     ax[2].start()
-    final(0)
+    ax[1].one()
     ax[2].one()
+    ax[1].two()
+    ax[2].two()
+    ax[1].three()
+    ax[2].three()
     ax[1].four()
-    ax[2].two()
     final(1)
-    ax[2].three()
     ax[2].four()
     final(2)
-    out[...] = oacc[...]
+    out[...] = oacc[...].T
+    drained = {id(cp) for cp in gx.cp.values()}
     for cp in started:
         if id(cp) not in drained:
             cp.wait_send()
@@ -434,19 +459,17 @@
     block_keys,
     block_count,
 ):
-    turn = timesteps.astype(F32) * (math.pi / 2000.0)
-    angles = jnp.stack([jnp.cos(turn), jnp.sin(turn)])
     smem = pl.BlockSpec(memory_space=pltpu.SMEM)
     hbm = pl.BlockSpec(memory_space=pl.ANY)
     dma = pltpu.SemaphoreType.DMA
     return pl.pallas_call(
         kernel,
-        out_shape=jax.ShapeDtypeStruct((ROWS, SLICE), F32),
+        out_shape=jax.ShapeDtypeStruct((SLICE, ROWS), F32),
         in_specs=[smem] * 4 + [hbm] * 5,
         out_specs=pl.BlockSpec(memory_space=pltpu.VMEM),
         scratch_shapes=[
             pltpu.VMEM((ROWS, D), BF16),
-            pltpu.VMEM((D, SLICE), BF16),
+            pltpu.VMEM((SLICE, D), BF16),
             pltpu.VMEM((ROWS, D), BF16),
             pltpu.VMEM((NX, NY, ROWS, SLICE), BF16),
             pltpu.VMEM((HEADS_HERE, NZ, 2, SLICE, ROWS), BF16),
@@ -471,9 +494,9 @@
             collective_id=0, has_side_effects=True, vmem_limit_bytes=67043328
         ),
     )(
-        angles, qk_gain, block_keys, block_count,
-        hidden_rows, gen_weight, noise, qkv_weight, out_weight,
-    )
+        timesteps, qk_gain, block_keys, block_count,
+        hidden_rows, gen_weight.T, noise, qkv_weight, out_weight,
+    ).T
 
 
 def solution(mesh):

time: 184 us -> 149 us (0.81)
  Pallas kernels: 173 us -> 147 us
  local copies, waits for them, and re-layouts: 7.88 us -> 1.84 us
    pallas_call x1, Pallas kernels: 173 us -> 147 us  [per_device(): pl.pallas_call(kernel, out_shape=jax.ShapeDtypeStruct((SLICE, ROWS), F32)...]
    unnamed x1, local copies, waits for them, and re-layouts: 5.82 us -> 1.84 us
    pallas_call x1 -> x0, local copies, waits for them, and re-layouts: 2.06 us -> none  [per_device(): pl.pallas_call(kernel, out_shape=jax.ShapeDtypeStruct((ROWS, SLICE), F32)...]
where the time goes in v2:
time: 149 us
  Pallas kernels  147 us (99%)
  local copies, waits for them, and re-layouts  1.84 us (1%)
    pallas_call x1, Pallas kernels, per_device(): pl.pallas_call(kernel, out_shape=jax.ShapeDtypeStruct((SLICE, ROWS), F32)...  147 us

profile of v2, /device:TPU:2, one launch (start us, length us, event | category | flops | bytes accessed | tf_op | source)
XLA Modules:
  0.0 148.6 jit_solution(5405613808325177384)
XLA Ops:
  0.0 146.7 %shard_map.91 = f32[320,384]{1,0:T(8,128)} custom-call(s32[6]{0:T(128)} %steps.1, f32[1,2,3]{2,1,0:T(2,128)} %gain.1, s32[3,6,8]{2,1,0:T(8,128)} %keys.1, s32[3,6]{1,0:T(4,128)} %count.1, bf16[384,5120]{1,0:T(8,128)(2,1)} %hidden.1, bf16[320,5120]{1,0:T(8,128)(2,1)} %bitcast.2, bf16[384,5120]{1,0:T(8,128)(2,1)} %noise.1, bf16[1,320,1152]{2,1,0:T(8,128)(2,1)} %qkv_w.1, ...), custom_call_target="tpu_custom_call" | custom-call | tf_op jit(solution)/shard_map/pallas_call | solution.py:465
  146.7 1.8 %copy.11 = f32[384,320]{0,1:T(8,128)} copy(f32[384,320]{0,1:T(8,128)} %bitcast.3) | data formatting | bytes 983040

commit v3 on v2

--- a/solution.py
+++ b/solution.py
@@ -56,6 +56,11 @@
 
     partner = {"seq": z * 2 + 1 - c}
 
+    barrier = pltpu.get_barrier_semaphore()
+    near = [at_z(1), at_z(-1), partner, at_x(1), at_x(-1), at_y(1), at_y(-1)]
+    for device in near:
+        pl.semaphore_signal(barrier, inc=1, device_id=device, device_id_type=MESH)
+
     def local(src, dst, i):
         cp = pltpu.make_async_copy(src, dst, loc_sem.at[i])
         cp.start()
@@ -69,17 +74,7 @@
     gw_cp = local(gen_w, gw, 4)
     nz_cp = local(noise, nz, 5)
 
-    barrier = pltpu.get_barrier_semaphore()
-    for d in (1, -1):
-        pl.semaphore_signal(barrier, inc=1, device_id=at_z(d), device_id_type=MESH)
-    pl.semaphore_signal(barrier, inc=1, device_id=partner, device_id_type=MESH)
-
-    def greet(i, carry):
-        pl.semaphore_signal(barrier, inc=1, device_id=plane(i), device_id_type=MESH)
-        return carry
-
-    lax.fori_loop(1, 16, greet, 0)
-    pl.semaphore_wait(barrier, 18)
+    pl.semaphore_wait(barrier, len(near))
 
     started = []
 
@@ -93,22 +88,25 @@
         return cp
 
     class Ring:
-        def __init__(self, g, part, whole):
+        def __init__(self, g, part, whole, own_part, own_whole):
             self.g, self.part, self.whole = g, part, whole
+            self.own_part, self.own_whole = own_part, own_whole
             self.cp = {}
 
         def push(self, way, half, k):
             shard = (z + NZ - way * (k - 1)) % NZ
             i = (0 if way > 0 else 7) + (k - 1 if half == 0 else (4 if way > 0 else 3) + k - 1)
             ref = self.part(shard, half)
+            src = self.own_part(half) if k == 1 else ref
             self.cp[way, half, k] = send(
-                ref, ref, zs.at[self.g, i], zr.at[self.g, i], at_z(way)
+                src, ref, zs.at[self.g, i], zr.at[self.g, i], at_z(way)
             )
 
         def give(self, d):
             ref = self.whole((z + d + NZ) % NZ)
             n = d + 3
-            self.cp["p", d] = send(ref, ref, ps.at[self.g, n], pr.at[self.g, n], partner)
+            src = self.own_whole() if d == 0 else ref
+            self.cp["p", d] = send(src, ref, ps.at[self.g, n], pr.at[self.g, n], partner)
 
         def own(self):
             self.push(1, 0, 1)
@@ -142,6 +140,8 @@
             h,
             lambda zz, half: wb.at[h, zz, c, pl.ds(half * 160, 160)],
             lambda zz: wb.at[h, zz, c],
+            lambda half: qkv_w.at[0, pl.ds(half * 160, 160), pl.ds(h * ROWS, ROWS)],
+            lambda: qkv_w.at[0, :, pl.ds(h * ROWS, ROWS)],
         )
 
     def kv_ring(h):
@@ -149,6 +149,8 @@
             3 + h,
             lambda zz, half: kv[h].at[zz, c, pl.ds(half * 3, 3)],
             lambda zz: kv[h].at[zz, c],
+            lambda half: kv[h].at[z, c, pl.ds(half * 3, 3)],
+            lambda: kv[h].at[z, c],
         )
 
     class Plane:
@@ -285,6 +287,7 @@
         lax.fori_loop(0, ROWS // BLOCK, norm_step, 0)
 
     def project(h):
+        w_own[h].wait()
         acc[...] = jnp.zeros((ROWS, ROWS), F32)
 
         def proj_step(zz, carry):
@@ -349,89 +352,87 @@
         lax.fori_loop(0, 4, final_step, 0)
 
     held = []
-    for h in range(HEADS_HERE):
-        w_own[h].wait()
     oacc[...] = jnp.zeros((ROWS, SLICE), F32)
     wr_[0].own()
+    wr_[0].step_a(1)
+    wr_[1].own()
     generate()
     gx.start()
+    wr_[0].step_b(1)
     cut()
-    wr_[0].step_a(1)
-    wr_[0].step_b(1)
-    wr_[1].own()
+    wr_[0].step_a(2)
+    wr_[1].step_a(1)
     gx.one()
-    wr_[0].step_a(2)
+    wr_[1].step_b(1)
     gx.two()
     wr_[0].step_b(2)
-    wr_[1].step_a(1)
-    wr_[1].step_b(1)
     wr_[0].step_a(3)
-    wr_[0].step_b(3)
     wr_[2].own()
     wr_[1].step_a(2)
+    wr_[1].step_b(2)
+    wr_[0].step_b(3)
     gx.three()
-    wr_[1].step_b(2)
     wr_[0].step_a(4)
     wr_[2].step_a(1)
     wr_[0].finish()
+    wr_[2].step_b(1)
     gx.four()
     norm()
     wr_[1].step_a(3)
     wr_[1].step_b(3)
-    wr_[2].step_b(1)
+    swap_start()
+    wr_[2].step_a(2)
     project(0)
-    wr_[2].step_a(2)
     kr_[0].own()
-    swap_start()
+    wr_[2].step_b(2)
     wr_[1].step_a(4)
-    wr_[2].step_b(2)
     wr_[2].step_a(3)
+    kr_[0].step_a(1)
+    kr_[0].step_b(1)
     wr_[1].finish()
     project(1)
-    kr_[0].step_a(1)
-    kr_[0].step_b(1)
+    wr_[2].step_a(4)
     kr_[1].own()
     wr_[2].step_b(3)
-    wr_[2].step_a(4)
     kr_[0].step_a(2)
     kr_[0].step_b(2)
     kr_[1].step_a(1)
+    kr_[1].step_b(1)
     wr_[2].finish()
     project(2)
+    kr_[2].own()
     kr_[0].step_a(3)
-    kr_[1].step_b(1)
-    kr_[2].own()
     kr_[0].step_b(3)
     kr_[1].step_a(2)
+    kr_[1].step_b(2)
+    kr_[2].step_a(1)
+    kr_[2].step_b(1)
     kr_[0].step_a(4)
-    kr_[1].step_b(2)
+    swap_end()
+    kr_[1].step_a(3)
     kr_[0].finish()
     attend(0)
-    kr_[2].step_a(1)
-    kr_[2].step_b(1)
+    kr_[1].step_b(3)
     ax[0].start()
-    kr_[1].step_a(3)
-    swap_end()
-    ax[0].one()
-    kr_[1].step_b(3)
-    ax[0].two()
     kr_[2].step_a(2)
     kr_[2].step_b(2)
+    ax[0].one()
     kr_[1].step_a(4)
     kr_[2].step_a(3)
-    ax[0].three()
+    ax[0].two()
     kr_[2].step_b(3)
     kr_[2].step_a(4)
-    ax[0].four()
-    held.pop().wait_recv()
-    final(0)
     kr_[1].finish()
     attend(1)
     ax[1].start()
+    ax[0].three()
     kr_[2].finish()
     attend(2)
     ax[2].start()
     ax[1].one()
+    ax[0].four()
+    held.pop().wait_recv()
+    final(0)
     ax[2].one()
     ax[1].two()
     ax[2].two()

time: 149 us -> 145 us (0.973)
  Pallas kernels: 147 us -> 143 us
    pallas_call x1, Pallas kernels: 147 us -> 143 us  [per_device(): pl.pallas_call(kernel, out_shape=jax.ShapeDtypeStruct((SLICE, ROWS), F32)...]
where the time goes in v3:
time: 145 us
  Pallas kernels  143 us (99%)
  local copies, waits for them, and re-layouts  1.84 us (1%)
    pallas_call x1, Pallas kernels, per_device(): pl.pallas_call(kernel, out_shape=jax.ShapeDtypeStruct((SLICE, ROWS), F32)...  143 us

profile of v3, /device:TPU:2, one launch (start us, length us, event | category | flops | bytes accessed | tf_op | source)
XLA Modules:
  0.0 145.2 jit_solution(346853138724460914)
XLA Ops:
  0.0 143.3 %shard_map.91 = f32[320,384]{1,0:T(8,128)} custom-call(s32[6]{0:T(128)} %steps.1, f32[1,2,3]{2,1,0:T(2,128)} %gain.1, s32[3,6,8]{2,1,0:T(8,128)} %keys.1, s32[3,6]{1,0:T(4,128)} %count.1, bf16[384,5120]{1,0:T(8,128)(2,1)} %hidden.1, bf16[320,5120]{1,0:T(8,128)(2,1)} %bitcast.2, bf16[384,5120]{1,0:T(8,128)(2,1)} %noise.1, bf16[1,320,1152]{2,1,0:T(8,128)(2,1)} %qkv_w.1, ...), custom_call_target="tpu_custom_call" | custom-call | tf_op jit(solution)/shard_map/pallas_call | solution.py:466
  143.3 1.8 %copy.11 = f32[384,320]{0,1:T(8,128)} copy(f32[384,320]{0,1:T(8,128)} %bitcast.3) | data formatting | bytes 983040

commit v4 on v3

--- a/solution.py
+++ b/solution.py
@@ -47,8 +47,8 @@
     def at_y(d):
         return {"head": (head // 4) * 4 + (y + d + NY) % NY}
 
-    def at_z(d):
-        return {"seq": ((z + d + NZ) % NZ) * 2 + c}
+    def at_z(d, core=c):
+        return {"seq": ((z + d + NZ) % NZ) * 2 + core}
 
     def plane(i):
         j = (me + i) % 16
@@ -101,6 +101,11 @@
             self.cp[way, half, k] = send(
                 src, ref, zs.at[self.g, i], zr.at[self.g, i], at_z(way)
             )
+            if k == 4 and self.g == 5:
+                n = 7 if way > 0 else 8
+                self.cp["p", 4, half] = send(
+                    ref, ref, ps.at[self.g, n], pr.at[self.g, n], at_z(way, 1 - c)
+                )
 
         def give(self, d):
             ref = self.whole((z + d + NZ) % NZ)
@@ -120,7 +125,7 @@
                 self.cp[way, half, k].wait_recv()
                 if k < 4:
                     self.push(way, half, k + 1)
-            if k == 4:
+            if k == 4 and self.g < 5:
                 self.give(4)
 
         def step_b(self, k):
@@ -132,8 +137,10 @@
             self.give(k)
 
         def finish(self):
-            for d in range(-3, 5):
+            for d in range(-3, 4):
                 self.cp["p", d].wait_recv()
+            for key in (("p", 4),) if self.g < 5 else (("p", 4, 0), ("p", 4, 1)):
+                self.cp[key].wait_recv()
 
     def w_ring(h):
         return Ring(
@@ -183,27 +190,31 @@
             b = self.buf
             for d in (1, -1):
                 self.cp["a2", d].wait_recv()
-            for d in (1, -1):
-                self.push(("a3", d), b.at[:, y, pl.ds(0, 192)], at_y(d))
+            for n in (0, 1):
+                for d, m in ((1, n), (-1, 1 - n)):
+                    self.push(("a3", d, n), b.at[pl.ds(2 * m, 2), y, pl.ds(0, 192)], at_y(d))
             for d in (1, -1):
                 self.cp["b2", d].wait_recv()
-            for d in (1, -1):
-                self.push(("b3", d), b.at[x, :, pl.ds(192, 192)], at_x(d))
+            for n in (0, 1):
+                for d, m in ((1, n), (-1, 1 - n)):
+                    self.push(("b3", d, n), b.at[x, pl.ds(2 * m, 2), pl.ds(192, 192)], at_x(d))
 
         def three(self):
             b = self.buf
             for n, d in enumerate((1, -1)):
-                self.cp["a3", d].wait_recv()
+                self.cp["a3", d, 0].wait_recv()
                 self.push(
                     ("a4", d), b.at[pl.ds(2 * n, 2), (y - d + NY) % NY, pl.ds(0, 192)], at_y(d)
                 )
-                self.cp["b3", d].wait_recv()
+                self.cp["b3", d, 0].wait_recv()
                 self.push(
                     ("b4", d), b.at[(x - d + NX) % NX, pl.ds(2 * n, 2), pl.ds(192, 192)], at_x(d)
                 )
 
         def four(self):
             for d in (1, -1):
+                self.cp["a3", d, 1].wait_recv()
+                self.cp["b3", d, 1].wait_recv()
                 self.cp["a4", d].wait_recv()
                 self.cp["b4", d].wait_recv()
 
@@ -484,10 +495,10 @@
             dma((8,)),
             dma((6, 14)),
             dma((6, 14)),
-            dma((6, 8)),
-            dma((6, 8)),
-            dma((4, 16)),
-            dma((4, 16)),
+            dma((6, 9)),
+            dma((6, 9)),
+            dma((4, 20)),
+            dma((4, 20)),
             dma((16,)),
             dma((16,)),
         ],

time: 145 us -> 144 us (level)
  no operation moved by 1% of the time
where the time goes in v4:
time: 144 us
  Pallas kernels  142 us (99%)
  local copies, waits for them, and re-layouts  1.84 us (1%)
    pallas_call x1, Pallas kernels, per_device(): pl.pallas_call(kernel, out_shape=jax.ShapeDtypeStruct((SLICE, ROWS), F32)...  142 us

profile of v4, /device:TPU:2, one launch (start us, length us, event | category | flops | bytes accessed | tf_op | source)
XLA Modules:
  0.0 143.8 jit_solution(3221449962778826808)
XLA Ops:
  0.0 142.0 %shard_map.91 = f32[320,384]{1,0:T(8,128)} custom-call(s32[6]{0:T(128)} %steps.1, f32[1,2,3]{2,1,0:T(2,128)} %gain.1, s32[3,6,8]{2,1,0:T(8,128)} %keys.1, s32[3,6]{1,0:T(4,128)} %count.1, bf16[384,5120]{1,0:T(8,128)(2,1)} %hidden.1, bf16[320,5120]{1,0:T(8,128)(2,1)} %bitcast.2, bf16[384,5120]{1,0:T(8,128)(2,1)} %noise.1, bf16[1,320,1152]{2,1,0:T(8,128)(2,1)} %qkv_w.1, ...), custom_call_target="tpu_custom_call" | custom-call | tf_op jit(solution)/shard_map/pallas_call | solution.py:477
  142.0 1.8 %copy.11 = f32[384,320]{0,1:T(8,128)} copy(f32[384,320]{0,1:T(8,128)} %bitcast.3) | data formatting | bytes 983040

commit v5 on v4

--- a/solution.py
+++ b/solution.py
@@ -211,10 +211,13 @@
                     ("b4", d), b.at[(x - d + NX) % NX, pl.ds(2 * n, 2), pl.ds(192, 192)], at_x(d)
                 )
 
-        def four(self):
+        def rest(self):
             for d in (1, -1):
                 self.cp["a3", d, 1].wait_recv()
                 self.cp["b3", d, 1].wait_recv()
+
+        def four(self):
+            for d in (1, -1):
                 self.cp["a4", d].wait_recv()
                 self.cp["b4", d].wait_recv()
 
@@ -363,6 +366,18 @@
         lax.fori_loop(0, 4, final_step, 0)
 
     held = []
+    def final_at(h, off):
+        top, low = pl.ds(0, 192), pl.ds(192, 192)
+        for p in (0, 2):
+            yy = (y + off) % NY
+            a = jnp.concatenate([at[h, p, yy, top, :], at[h, p + 1, yy, top, :]], axis=-1)
+            w = jnp.concatenate([wo[h, p * NY + yy], wo[h, (p + 1) * NY + yy]], axis=0)
+            oacc[top, :] += jnp.dot(a, w, preferred_element_type=F32)
+            xx = (x + off) % NX
+            a = jnp.concatenate([at[h, xx, p, low, :], at[h, xx, p + 1, low, :]], axis=-1)
+            w = wo[h, pl.ds(xx * NY + p, 2)].reshape(256, SLICE)
+            oacc[low, :] += jnp.dot(a, w, preferred_element_type=F32)
+
     oacc[...] = jnp.zeros((ROWS, SLICE), F32)
     wr_[0].own()
     wr_[0].step_a(1)
@@ -387,6 +402,7 @@
     wr_[2].step_a(1)
     wr_[0].finish()
     wr_[2].step_b(1)
+    gx.rest()
     gx.four()
     norm()
     wr_[1].step_a(3)
@@ -441,6 +457,7 @@
     attend(2)
     ax[2].start()
     ax[1].one()
+    ax[0].rest()
     ax[0].four()
     held.pop().wait_recv()
     final(0)
@@ -449,10 +466,15 @@
     ax[2].two()
     ax[1].three()
     ax[2].three()
+    final_at(2, 0)
+    ax[2].rest()
+    final_at(2, 1)
+    final_at(2, 3)
+    ax[1].rest()
     ax[1].four()
     final(1)
     ax[2].four()
-    final(2)
+    final_at(2, 2)
     out[...] = oacc[...].T
     drained = {id(cp) for cp in gx.cp.values()}
     for cp in started:

time: 144 us -> 143 us (level)
  no operation moved by 1% of the time
where the time goes in v5:
time: 143 us
  Pallas kernels  141 us (99%)
  local copies, waits for them, and re-layouts  1.84 us (1%)
    pallas_call x1, Pallas kernels, per_device(): pl.pallas_call(kernel, out_shape=jax.ShapeDtypeStruct((SLICE, ROWS), F32)...  141 us

profile of v5, /device:TPU:2, one launch (start us, length us, event | category | flops | bytes accessed | tf_op | source)
XLA Modules:
  0.0 142.6 jit_solution(15487820063757413326)
XLA Ops:
  0.0 140.8 %shard_map.91 = f32[320,384]{1,0:T(8,128)} custom-call(s32[6]{0:T(128)} %steps.1, f32[1,2,3]{2,1,0:T(2,128)} %gain.1, s32[3,6,8]{2,1,0:T(8,128)} %keys.1, s32[3,6]{1,0:T(4,128)} %count.1, bf16[384,5120]{1,0:T(8,128)(2,1)} %hidden.1, bf16[320,5120]{1,0:T(8,128)(2,1)} %bitcast.2, bf16[384,5120]{1,0:T(8,128)(2,1)} %noise.1, bf16[1,320,1152]{2,1,0:T(8,128)(2,1)} %qkv_w.1, ...), custom_call_target="tpu_custom_call" | custom-call | tf_op jit(solution)/shard_map/pallas_call | solution.py:499
  140.8 1.8 %copy.11 = f32[384,320]{0,1:T(8,128)} copy(f32[384,320]{0,1:T(8,128)} %bitcast.3) | data formatting | bytes 983040

commit v6 on v5

--- a/solution.py
+++ b/solution.py
@@ -427,9 +427,9 @@
     kr_[1].step_b(1)
     wr_[2].finish()
     project(2)
-    kr_[2].own()
     kr_[0].step_a(3)
     kr_[0].step_b(3)
+    kr_[2].own()
     kr_[1].step_a(2)
     kr_[1].step_b(2)
     kr_[2].step_a(1)

time: 143 us -> 143 us (level)
  no operation moved by 1% of the time
where the time goes in v6:
time: 143 us
  Pallas kernels  141 us (99%)
  local copies, waits for them, and re-layouts  1.84 us (1%)
    pallas_call x1, Pallas kernels, per_device(): pl.pallas_call(kernel, out_shape=jax.ShapeDtypeStruct((SLICE, ROWS), F32)...  141 us

profile of v6, /device:TPU:2, one launch (start us, length us, event | category | flops | bytes accessed | tf_op | source)
XLA Modules:
  0.0 142.6 jit_solution(1346685228638505722)
XLA Ops:
  0.0 140.8 %shard_map.91 = f32[320,384]{1,0:T(8,128)} custom-call(s32[6]{0:T(128)} %steps.1, f32[1,2,3]{2,1,0:T(2,128)} %gain.1, s32[3,6,8]{2,1,0:T(8,128)} %keys.1, s32[3,6]{1,0:T(4,128)} %count.1, bf16[384,5120]{1,0:T(8,128)(2,1)} %hidden.1, bf16[320,5120]{1,0:T(8,128)(2,1)} %bitcast.2, bf16[384,5120]{1,0:T(8,128)(2,1)} %noise.1, bf16[1,320,1152]{2,1,0:T(8,128)(2,1)} %qkv_w.1, ...), custom_call_target="tpu_custom_call" | custom-call | tf_op jit(solution)/shard_map/pallas_call | solution.py:499
  140.8 1.8 %copy.11 = f32[384,320]{0,1:T(8,128)} copy(f32[384,320]{0,1:T(8,128)} %bitcast.3) | data formatting | bytes 983040
